TPU v7x, 32 devices: a whole 2x2x4 slice. The times are simulated.
32 devices in a mesh: rows: 16 (over z, x, core), split: 2 (over y).
Axes of the slice: x: 2, y: 2, z: 4, core: 2. Of those that a mesh axis runs over, the one named last changes fastest.
Arguments:
- embeddings: bfloat16 [8192, 768], P(('rows', 'split')), may hold values from -24 to 24
- cluster_id: int32 [8192], P(('rows', 'split')), may hold values from 0 to 127, as said below
- owner_map: int32 [128], replicated, may hold values from 0 to 15, as said below
Outputs:
- prune_score: float32 [8192], P(('rows', 'split'))
Inputs may be any that keep to these rules, and one draw needn't show every extreme that they name: `owner_map`: every group 0 to 15 holds exactly 8 clusters. `cluster_id`: within each aligned block of 256 rows (the rows of one device), no group holds more than 32 of the block's rows, and one group holds exactly 32; every group holds exactly 32 rows of some block. Every cluster holds two rows or more.
All inputs are finite; a program needn't handle non-finite values.
Results may differ from a plain program's by a relative error of at most 0.0005.
Values may be sent and summed in bfloat16 or wider, within the bound.
A program may use at most 64 MiB of HBM per device.

v0:
```python
import jax
import jax.numpy as jnp
from jax import lax
from jax.sharding import PartitionSpec as P

FLOOR_SCORE = -1e30


def block_logsumexp(queries, key_rows, allowed):
    score_scale = 1.0 / queries.shape[1] ** 0.5
    scores = (
        jnp.einsum("qd,kd->qk", queries, key_rows, preferred_element_type=jnp.float32) * score_scale
    )
    masked = jnp.where(allowed, scores, FLOOR_SCORE)
    highest = jnp.max(masked, axis=1)
    totals = jnp.sum(jnp.where(allowed, jnp.exp(masked - highest[:, None]), 0.0), axis=1)
    return (highest, totals)


def merge_pair(earlier_pair, later_pair):
    highest = jnp.maximum(earlier_pair[0], later_pair[0])
    totals = later_pair[1] * jnp.exp(later_pair[0] - highest)
    return (highest, totals)


def cluster_means(density, member_ids, clusters_all):
    present = member_ids >= 0
    segment = jnp.where(present, member_ids, clusters_all)
    sum_density = jax.ops.segment_sum(jnp.where(present, density, 0.0), segment, clusters_all + 1)[
        :clusters_all
    ]
    counts = jax.ops.segment_sum(present.astype(jnp.float32), segment, clusters_all + 1)[
        :clusters_all
    ]
    return (sum_density, counts)


def on_device(embeddings, cluster_id, owner_map):
    rows_here = embeddings.shape[0]
    width = embeddings.shape[1]
    clusters_all = owner_map.shape[0]
    owners_count = lax.axis_size("rows")
    capacity = 2 * rows_here // owners_count
    slot_count = owners_count * capacity
    cluster_range = jnp.arange(clusters_all, dtype=jnp.int32)
    table_hit = cluster_id[:, None] == cluster_range[None, :]
    owner_of = jnp.sum(jnp.where(table_hit, owner_map[None, :], 0), axis=1)
    same_owner = owner_of[:, None] == owner_of[None, :]
    earlier = jnp.arange(rows_here)[None, :] < jnp.arange(rows_here)[:, None]
    ranking = jnp.sum(same_owner & earlier, axis=1)
    slot_index = owner_of * capacity + ranking
    placed = jnp.arange(slot_count, dtype=jnp.int32)[:, None] == slot_index[None, :]
    outgoing = jnp.dot(
        placed.astype(jnp.bfloat16), embeddings, preferred_element_type=jnp.float32
    ).astype(jnp.bfloat16)
    out_ids = jnp.sum(jnp.where(placed, cluster_id[None, :] + 1, 0), axis=1) - 1
    arrived, arrived_ids = (
        lax.all_to_all(
            outgoing.reshape(owners_count, capacity, width),
            "rows",
            split_axis=0,
            concat_axis=0,
            tiled=True,
        ),
        lax.all_to_all(
            out_ids.reshape(owners_count, capacity), "rows", split_axis=0, concat_axis=0, tiled=True
        ),
    )
    key_rows = arrived.reshape(slot_count, width)
    key_ids = arrived_ids.reshape(slot_count)
    piece_index = lax.axis_index("split")
    my_start = piece_index * slot_count
    positions = my_start + jnp.arange(slot_count, dtype=jnp.int32)
    initial = (
        jnp.full((slot_count,), FLOOR_SCORE, jnp.float32),
        jnp.zeros((slot_count,), jnp.float32),
    )
    portion_rows = lax.all_gather(key_rows, "split", axis=0, tiled=True)
    portion_ids = lax.all_gather(key_ids, "split", axis=0, tiled=True)
    length = portion_ids.shape[0]
    key_positions = jnp.arange(length, dtype=jnp.int32)
    allowed = (
        (portion_ids[None, :] >= 0)
        & (portion_ids[None, :] == key_ids[:, None])
        & (positions[:, None] != key_positions[None, :])
    )
    highest, totals = merge_pair(initial, block_logsumexp(key_rows, portion_rows, allowed))
    density = highest + jnp.log(totals)
    sum_density, counts = cluster_means(density, key_ids, clusters_all)
    sum_density, counts = lax.psum((sum_density, counts), "split")
    cluster_mean = sum_density / jnp.maximum(counts, 1.0)
    row_hit = key_ids[:, None] == cluster_range[None, :]
    row_mean = jnp.sum(jnp.where(row_hit, cluster_mean[None, :], 0.0), axis=1)
    slot_score = jnp.where(key_ids >= 0, density - row_mean, 0.0)
    returned = lax.all_to_all(
        slot_score.reshape(owners_count, capacity), "rows", split_axis=0, concat_axis=0, tiled=True
    )
    returned_flat = returned.reshape(slot_count)
    return jnp.sum(jnp.where(placed, returned_flat[:, None], 0.0), axis=0)


def solution(mesh):
    placed = (P(("rows", "split"), None), P(("rows", "split")), P())
    return jax.shard_map(
        on_device, mesh=mesh, in_specs=placed, out_specs=P(("rows", "split")), check_vma=False
    )
```

profile of v0, /device:TPU:0, one launch (start us, length us, event | category | flops | bytes accessed | tf_op | source)
XLA Modules:
  0.0 97.4 jit_solution(236340904709516073)
XLA Ops:
  6.5 0.9 select_reduce_fusion.4
  7.5 0.2 convert_reduce_fusion
  7.6 0.7 multiply_add_fusion
  8.3 0.4 convolution_convert_fusion
  8.7 27.4 %all_to_all.17 = bf16[16,32,768]{2,1,0:T(8,128)(2,1)} all-to-all(bf16[16,32,768]{2,1,0:T(8,128)(2,1)S(1)} %bitcast.10), channel_id=1, replica_groups=mesh['rows'=16,'split'=2] {'rows'}, dimensions={0} | all-to-all | bytes 1572864 | tf_op jit(solution)/shard_map/all_to_all | solution.py:58
  36.2 0.1 select_reduce_fusion.2
  36.3 0.7 sub.39
  37.0 3.9 %all-to-all-start = ((s32[16,1,32]{2,1,0:T(1,128)}), s32[16,1,32]{2,1,0:T(1,128)S(1)}, u32[]{:S(2)}, u32[]{:S(2)}) async-start(s32[16,1,32]{2,1,0:T(1,128)} %sub.39), calls=%async_computation | async-start | bytes 16384 | tf_op jit(solution)/shard_map/all_to_all | solution.py:65
  41.0 6.4 %all-to-all-done = s32[16,1,32]{2,1,0:T(1,128)S(1)} async-done(((s32[16,1,32]{2,1,0:T(1,128)}), s32[16,1,32]{2,1,0:T(1,128)S(1)}, u32[]{:S(2)}, u32[]{:S(2)}) %all-to-all-start) | async-done | bytes 2080 | tf_op jit(solution)/shard_map/all_to_all | solution.py:65
  47.5 0.5 broadcast.91
  48.0 0.7 reduce.10
  48.8 4.1 %scatter_custom_fusion.1 = f32[129]{0:T(256)S(1)} fusion(s32[512]{0:T(512)S(1)} %bitcast.16, f32[512]{0:T(512)S(1)} %get-tuple-element.7, f32[]{:T(128)} %constant.6.clone.1), kind=kCustom, calls=%fused_computation.38 | custom fusion | flops 512 | bytes 520 | tf_op jit(solution)/shard_map/scatter-add | solution.py:32
  52.9 4.5 %all-gather = s32[2,1,512]{2,1,0:T(1,128)S(1)} all-gather(s32[1,1,512]{2,1,0:T(1,128)S(1)} %reshape.147), channel_id=1, replica_groups=mesh['rows'=16,'split'=2] {'split'}, dimensions={0}, use_global_device_ids=true | all-gather | bytes 6144 | tf_op jit(solution)/shard_map/all_gather | solution.py:79
  57.5 5.4 %all-gather.3.cloned.1.call-done = bf16[1024,768]{1,0:T(8,128)(2,1)} async-done(((bf16[512,768]{1,0:T(8,128)(2,1)}), bf16[1024,768]{1,0:T(8,128)(2,1)}) %all-gather.3.cloned.1.call-update) | async-done | bytes 1572880 | tf_op jit(solution)/shard_map/all_gather | solution.py:78
  62.9 3.1 %fusion.1 = (f32[512]{0:T(512)S(1)}, f32[512,1024]{1,0:T(8,128)S(1)}) fusion(s32[512]{0:T(512)S(1)} %iota_add_fusion, s32[1024]{0:T(1024)S(1)} %bitcast.14, s32[512]{0:T(512)S(1)} %reshape.127, pred[1024]{0:T(1024)(128)(4,1)S(1)} %broadcast_compare_fusion, bf16[512,768]{1,0:T(8,128)(2,1)} %bitcast.9, bf16[1024,768]{1,0:T(8,128)(2,1)} %all-gather.3.cloned.1.call-done), kind=kOutput, calls=%fused_computation.6 | convolution fusion | flops 808975872 | bytes 4467712 | tf_op jit(solution)/shard_map/qd,kd->qk/dot_general | solution.py:12
  66.0 1.2 %select_reduce_fusion = f32[512]{0:T(512)S(1)} fusion(f32[512,1024]{1,0:T(8,128)S(1)} %get-tuple-element.10, f32[512]{0:T(512)S(1)} %get-tuple-element.9, s32[512]{0:T(512)S(1)} %iota_add_fusion, s32[1024]{0:T(1024)S(1)} %bitcast.15, s32[512]{0:T(512)S(1)} %reshape.127, pred[1024]{0:T(1024)(128)(4,1)S(1)} %broadcast_compare_fusion), kind=kLoop, calls=%fused_computation.2 | loop fusion | flops 4718080 | bytes 2110464 | tf_op jit(solution)/shard_map/reduce_sum | solution.py:16
  67.2 0.1 reduce_sum.62
  67.3 4.1 %scatter_custom_fusion = f32[129]{0:T(256)S(1)} fusion(s32[512]{0:T(512)S(1)} %bitcast.17, f32[512]{0:T(512)S(1)} %fusion.10, f32[]{:T(128)} %constant.6.clone.1), kind=kCustom, calls=%fused_computation.40 | custom fusion | flops 512 | bytes 520 | tf_op jit(solution)/shard_map/scatter-add | solution.py:29
  71.4 4.9 %all-reduce = (f32[128]{0:T(128)S(1)}, f32[128]{0:T(128)S(1)}) all-reduce(f32[128]{0:T(128)S(1)} %slice.6, f32[128]{0:T(128)S(1)} %slice-done), channel_id=1, replica_groups=mesh['rows'=16,'split'=2] {'split'}, use_global_device_ids=true, to_apply=%region_6.7 | all-reduce | flops 256 | bytes 2048 | tf_op jit(solution)/shard_map/psum | solution.py:90
  76.4 0.2 select_reduce_fusion.3
  76.7 11.9 %all_to_all.18 = f32[16,1,32]{2,1,0:T(1,128)S(1)} all-to-all(f32[16,1,32]{2,1,0:T(1,128)S(1)} %compare_select_fusion), channel_id=1, replica_groups=mesh['rows'=16,'split'=2] {'rows'}, dimensions={0} | all-to-all | bytes 4096 | tf_op jit(solution)/shard_map/all_to_all | solution.py:95
  88.6 0.5 broadcast.92
  89.1 0.7 reduce.11
  89.9 0.7 select_reduce_fusion.1
  (23 shorter events, 0.6 us)
Async XLA Ops:
  6.5 1.8 %copy-start = (bf16[256,768]{1,0:T(8,128)(2,1)S(1)}, bf16[256,768]{1,0:T(8,128)(2,1)}, u32[]{:S(2)}) copy-start(bf16[256,768]{1,0:T(8,128)(2,1)} %param.3) | copy-start | bytes 1179652
  6.5 56.3 %all-gather.3.cloned.1.call-start = ((), (), s32[]{:S(2)}) async-start(), calls=%async_computation.3 | async-start | bytes 2359296 | tf_op jit(solution)/shard_map/all_gather | solution.py:78
  37.0 10.4 %all-to-all-start = ((s32[16,1,32]{2,1,0:T(1,128)}), s32[16,1,32]{2,1,0:T(1,128)S(1)}, u32[]{:S(2)}, u32[]{:S(2)}) async-start(s32[16,1,32]{2,1,0:T(1,128)} %sub.39), calls=%async_computation | async-start | bytes 16384 | tf_op jit(solution)/shard_map/all_to_all | solution.py:65
  52.9 13.0 %copy-start.1 = (f32[129]{0:T(256)}, f32[129]{0:T(256)S(1)}, u32[]{:S(2)}) copy-start(f32[129]{0:T(256)S(1)} %scatter_custom_fusion.1) | copy-start | bytes 1552
  65.9 5.5 %slice-start = ((f32[129]{0:T(256)}), f32[128]{0:T(128)S(1)}, s32[]{:S(2)}) async-start(f32[129]{0:T(256)} %copy-done.1), calls=%async_computation.4 | async-start | bytes 1024 | tf_op jit(solution)/shard_map/slice | solution.py:32
Sparse Core Ops, SparseCore 0:
  36.3 26.5 all-gather.2
where the time goes:
time: 97.8 us; the launch traced here: 97.4 us
  blocking collectives  48.7 us (50%)
  other arithmetic  13.7 us (14%)
  between operations  13.5 us (14%)
  waiting for transfers between devices  11.8 us (12%)
  starting transfers between devices  3.94 us (4%)
  matrix products  3.43 us (4%)
  local copies, waits for them, and re-layouts  2.3 us (2%)
    all_to_all x1, blocking collectives, on_device(): lax.all_to_all(outgoing.reshape(owners_count, capacity, width), 'rows', s...  27.4 us
    all_to_all x1, blocking collectives, on_device(): lax.all_to_all(slot_score.reshape(owners_count, capacity), 'rows', split_...  11.9 us
    all_to_all x1, waiting for transfers between devices, on_device(): lax.all_to_all(out_ids.reshape(owners_count, capacity), 'rows', split_axi...  6.42 us
    all_gather x1, waiting for transfers between devices, on_device(): portion_rows = lax.all_gather(key_rows, 'split', axis=0, tiled=True)  5.4 us
    psum x1, blocking collectives, on_device(): sum_density, counts = lax.psum((sum_density, counts), 'split')  4.93 us
    all_gather x1, blocking collectives, on_device(): portion_ids = lax.all_gather(key_ids, 'split', axis=0, tiled=True)  4.54 us
    scatter-add x1, other arithmetic, cluster_means(): jax.ops.segment_sum(jnp.where(present, density, 0.0), segment, clusters_a...  4.09 us
    scatter-add x1, other arithmetic, cluster_means(): jax.ops.segment_sum(present.astype(jnp.float32), segment, clusters_all + 1)  4.09 us
  transfers between devices with their start and end apart: 2, of which 2 were waited for; matrix products, arithmetic and copies ran while one was open for 7% of the time, Pallas kernels for 0%

commit v1 on v0

--- a/solution.py
+++ b/solution.py
@@ -4,6 +4,18 @@
 from jax.sharding import PartitionSpec as P
 
 FLOOR_SCORE = -1e30
+
+
+def gather_by_bits(value, axis, dim):
+    ways, here = (lax.axis_size(axis), lax.axis_index(axis))
+    grown, reach = (value, 1)
+    while reach < ways:
+        theirs = lax.ppermute(grown, axis, [(d, d ^ reach) for d in range(ways)])
+        mine_first = jnp.concatenate([grown, theirs], axis=dim)
+        theirs_first = jnp.concatenate([theirs, grown], axis=dim)
+        grown = jnp.where(here & reach == 0, mine_first, theirs_first)
+        reach = 2 * reach
+    return grown
 
 
 def block_logsumexp(queries, key_rows, allowed):
@@ -75,7 +87,7 @@
         jnp.full((slot_count,), FLOOR_SCORE, jnp.float32),
         jnp.zeros((slot_count,), jnp.float32),
     )
-    portion_rows = lax.all_gather(key_rows, "split", axis=0, tiled=True)
+    portion_rows = gather_by_bits(key_rows, "split", 0)
     portion_ids = lax.all_gather(key_ids, "split", axis=0, tiled=True)
     length = portion_ids.shape[0]
     key_positions = jnp.arange(length, dtype=jnp.int32)

time: 97.8 us -> 82.6 us (0.84)
  blocking collectives: 48.7 us -> 24.9 us
  between operations: 13.5 us -> 0.11 us
  waiting for transfers between devices: 11.8 us -> 22.7 us
  starting transfers between devices: 3.94 us -> 14.3 us
    all_to_all x1 -> x0, blocking collectives: 27.4 us -> none  [on_device(): lax.all_to_all(outgoing.reshape(owners_count, capacity, width), 'rows', s...]
    all_to_all x0 -> x1, waiting for transfers between devices: none -> 17.8 us  [on_device(): lax.all_to_all(outgoing.reshape(owners_count, capacity, width), 'rows', s...]
    all_to_all x0 -> x1, starting transfers between devices: none -> 7.38 us  [on_device(): lax.all_to_all(outgoing.reshape(owners_count, capacity, width), 'rows', s...]
    all_gather x1 -> x0, waiting for transfers between devices: 5.4 us -> none  [on_device(): portion_rows = lax.all_gather(key_rows, 'split', axis=0, tiled=True)]
    all_gather x1, blocking collectives: 4.54 us -> 8.04 us  [on_device(): portion_ids = lax.all_gather(key_ids, 'split', axis=0, tiled=True)]
    ppermute x0 -> x1, starting transfers between devices: none -> 1.58 us  [gather_by_bits(): theirs = lax.ppermute(grown, axis, [(d, d ^ reach) for d in range(ways)])]
    all_to_all x1, waiting for transfers between devices: 6.42 us -> 4.85 us  [on_device(): lax.all_to_all(out_ids.reshape(owners_count, capacity), 'rows', split_axi...]
    all_to_all x1, starting transfers between devices: 3.93 us -> 5.38 us  [on_device(): lax.all_to_all(out_ids.reshape(owners_count, capacity), 'rows', split_axi...]
  transfers between devices with their start and end apart: 2 -> 3, of which waited for: 2 -> 2; matrix products, arithmetic and copies ran while one was open for 7% -> 8% of each run, Pallas kernels for 0% -> 0%
where the time goes in v1:
time: 82.6 us; the launch traced here: 82.2 us
  blocking collectives  24.9 us (30%)
  waiting for transfers between devices  22.7 us (27%)
  starting transfers between devices  14.3 us (17%)
  other arithmetic  13.7 us (17%)
  matrix products  4.16 us (5%)
  local copies, waits for them, and re-layouts  2.3 us (3%)
    all_to_all x1, waiting for transfers between devices, on_device(): lax.all_to_all(outgoing.reshape(owners_count, capacity, width), 'rows', s...  17.8 us
    all_to_all x1, blocking collectives, on_device(): lax.all_to_all(slot_score.reshape(owners_count, capacity), 'rows', split_...  12 us
    all_gather x1, blocking collectives, on_device(): portion_ids = lax.all_gather(key_ids, 'split', axis=0, tiled=True)  8.04 us
    all_to_all x1, starting transfers between devices, on_device(): lax.all_to_all(outgoing.reshape(owners_count, capacity, width), 'rows', s...  7.38 us
    all_to_all x1, starting transfers between devices, on_device(): lax.all_to_all(out_ids.reshape(owners_count, capacity), 'rows', split_axi...  5.38 us
    psum x1, blocking collectives, on_device(): sum_density, counts = lax.psum((sum_density, counts), 'split')  4.93 us
    all_to_all x1, waiting for transfers between devices, on_device(): lax.all_to_all(out_ids.reshape(owners_count, capacity), 'rows', split_axi...  4.85 us
    scatter-add x1, other arithmetic, cluster_means(): jax.ops.segment_sum(jnp.where(present, density, 0.0), segment, clusters_a...  4.09 us
  transfers between devices with their start and end apart: 3, of which 2 were waited for; matrix products, arithmetic and copies ran while one was open for 8% of the time, Pallas kernels for 0%

profile of v1, /device:TPU:0, one launch (start us, length us, event | category | flops | bytes accessed | tf_op | source)
XLA Modules:
  0.0 82.2 jit_solution(18114208266629917843)
XLA Ops:
  0.0 0.9 %select_reduce_fusion.4 = s32[256]{0:T(256)S(1)} fusion(s32[128]{0:T(128)} %param.5, s32[256]{0:T(256)} %param.4), kind=kLoop, calls=%fused_computation.25 | loop fusion | flops 98048 | bytes 2560 | tf_op jit(solution)/shard_map/reduce_sum | solution.py:59
  0.9 0.2 convert_reduce_fusion
  1.1 0.7 multiply_add_fusion
  1.8 1.3 %convolution_convert_fusion = bf16[512,768]{1,0:T(8,128)(2,1)} fusion(bf16[256,768]{1,0:T(8,128)(2,1)S(1)} %copy-done, s32[256]{0:T(256)S(1)} %get-tuple-element.11), kind=kOutput, calls=%fused_computation.15 | convolution fusion | flops 201850880 | bytes 1180672 | tf_op jit(solution)/shard_map/dot_general | solution.py:65
  3.1 7.4 %all-to-all-start.1 = ((bf16[16,32,768]{2,1,0:T(8,128)(2,1)}), bf16[16,32,768]{2,1,0:T(8,128)(2,1)S(1)}, u32[]{:S(2)}, u32[]{:S(2)}) async-start(bf16[16,32,768]{2,1,0:T(8,128)(2,1)} %bitcast.1), calls=%async_computation.1 | async-start | bytes 1572864 | tf_op jit(solution)/shard_map/all_to_all | solution.py:70
  10.5 0.1 select_reduce_fusion.2
  10.6 0.7 sub.39
  11.3 17.8 %all-to-all-done.1 = bf16[16,32,768]{2,1,0:T(8,128)(2,1)S(1)} async-done(((bf16[16,32,768]{2,1,0:T(8,128)(2,1)}), bf16[16,32,768]{2,1,0:T(8,128)(2,1)S(1)}, u32[]{:S(2)}, u32[]{:S(2)}) %all-to-all-start.1) | async-done | bytes 786464 | tf_op jit(solution)/shard_map/all_to_all | solution.py:70
  29.1 5.4 %all-to-all-start = ((s32[16,1,32]{2,1,0:T(1,128)}), s32[16,1,32]{2,1,0:T(1,128)S(1)}, u32[]{:S(2)}, u32[]{:S(2)}) async-start(s32[16,1,32]{2,1,0:T(1,128)} %sub.39), calls=%async_computation | async-start | bytes 16384 | tf_op jit(solution)/shard_map/all_to_all | solution.py:77
  34.5 1.6 %collective-permute-start = (bf16[512,768]{1,0:T(8,128)(2,1)S(1)}, bf16[512,768]{1,0:T(8,128)(2,1)}, u32[]{:S(2)}, u32[]{:S(2)}) collective-permute-start(bf16[512,768]{1,0:T(8,128)(2,1)S(1)} %bitcast.7), channel_id=1, source_target_pairs={{0,1},{1,0},{2,3},{3,2},{4,5},{5,4},{6,7},{7,6},{8,9},{9,8},{10,11... | collective-permute-start | bytes 2359304 | tf_op jit(solution)/shard_map/ppermute | solution.py:13
  36.1 4.8 %all-to-all-done = s32[16,1,32]{2,1,0:T(1,128)S(1)} async-done(((s32[16,1,32]{2,1,0:T(1,128)}), s32[16,1,32]{2,1,0:T(1,128)S(1)}, u32[]{:S(2)}, u32[]{:S(2)}) %all-to-all-start) | async-done | bytes 2080 | tf_op jit(solution)/shard_map/all_to_all | solution.py:77
  41.1 0.5 broadcast.91
  41.6 0.7 reduce.10
  42.4 4.1 %scatter_custom_fusion.1 = f32[129]{0:T(256)S(1)} fusion(s32[512]{0:T(512)S(1)} %bitcast.14, f32[512]{0:T(512)S(1)} %get-tuple-element.7, f32[]{:T(128)} %constant.5.clone.1), kind=kCustom, calls=%fused_computation.46 | custom fusion | flops 512 | bytes 520 | tf_op jit(solution)/shard_map/scatter-add | solution.py:44
  46.5 8.0 %all-gather = s32[2,1,512]{2,1,0:T(1,128)S(1)} all-gather(s32[1,1,512]{2,1,0:T(1,128)S(1)} %reshape.147), channel_id=1, replica_groups=mesh['rows'=16,'split'=2] {'split'}, dimensions={0}, use_global_device_ids=true | all-gather | bytes 6144 | tf_op jit(solution)/shard_map/all_gather | solution.py:91
  54.5 2.9 %fusion.1 = (f32[512]{0:T(512)S(1)}, f32[512,1024]{1,0:T(8,128)S(1)}) fusion(s32[512]{0:T(512)S(1)} %iota_add_fusion, s32[1024]{0:T(1024)S(1)} %bitcast.12, s32[512]{0:T(512)S(1)} %reshape.127, pred[1024]{0:T(1024)(128)(4,1)S(1)} %broadcast_compare_fusion, bf16[512,768]{1,0:T(8,128)(2,1)S(1)} %bitcast.8, bf16[512,768]{1,0:T(8,128)(2,1)} %collective-permute-done, ...), kind=kOutput, calls=%fused_computation.6 | convolution fusion | flops 816053760 | bytes 3681281 | tf_op jit(solution)/shard_map/qd,kd->qk/dot_general | solution.py:24
  57.6 1.2 %select_reduce_fusion = f32[512]{0:T(512)S(1)} fusion(f32[512,1024]{1,0:T(8,128)S(1)} %get-tuple-element.10, f32[512]{0:T(512)S(1)} %get-tuple-element.9, s32[512]{0:T(512)S(1)} %iota_add_fusion, s32[1024]{0:T(1024)S(1)} %bitcast.13, s32[512]{0:T(512)S(1)} %reshape.127, pred[1024]{0:T(1024)(128)(4,1)S(1)} %broadcast_compare_fusion), kind=kLoop, calls=%fused_computation.2 | loop fusion | flops 4718080 | bytes 2110464 | tf_op jit(solution)/shard_map/reduce_sum | solution.py:28
  58.8 4.1 %scatter_custom_fusion = f32[129]{0:T(256)S(1)} fusion(s32[512]{0:T(512)S(1)} %bitcast.15, f32[512]{0:T(512)S(1)} %fusion.17, f32[]{:T(128)} %constant.5.clone.1), kind=kCustom, calls=%fused_computation.48 | custom fusion | flops 512 | bytes 520 | tf_op jit(solution)/shard_map/scatter-add | solution.py:41
  63.0 4.9 %all-reduce = (f32[128]{0:T(128)S(1)}, f32[128]{0:T(128)S(1)}) all-reduce(f32[128]{0:T(128)S(1)} %slice.6, f32[128]{0:T(128)S(1)} %slice-done), channel_id=1, replica_groups=mesh['rows'=16,'split'=2] {'split'}, use_global_device_ids=true, to_apply=%region_6.7 | all-reduce | flops 256 | bytes 2048 | tf_op jit(solution)/shard_map/psum | solution.py:102
  67.9 0.2 select_reduce_fusion.3
  68.3 12.0 %all_to_all.17 = f32[16,1,32]{2,1,0:T(1,128)S(1)} all-to-all(f32[16,1,32]{2,1,0:T(1,128)S(1)} %compare_select_fusion), channel_id=1, replica_groups=mesh['rows'=16,'split'=2] {'rows'}, dimensions={0} | all-to-all | bytes 4096 | tf_op jit(solution)/shard_map/all_to_all | solution.py:107
  80.2 0.5 broadcast.92
  80.7 0.7 reduce.11
  81.5 0.7 select_reduce_fusion.1
  (23 shorter events, 0.7 us)
Async XLA Ops:
  0.0 1.8 %copy-start = (bf16[256,768]{1,0:T(8,128)(2,1)S(1)}, bf16[256,768]{1,0:T(8,128)(2,1)}, u32[]{:S(2)}) copy-start(bf16[256,768]{1,0:T(8,128)(2,1)} %param.3) | copy-start | bytes 1179652
  3.1 26.1 %all-to-all-start.1 = ((bf16[16,32,768]{2,1,0:T(8,128)(2,1)}), bf16[16,32,768]{2,1,0:T(8,128)(2,1)S(1)}, u32[]{:S(2)}, u32[]{:S(2)}) async-start(bf16[16,32,768]{2,1,0:T(8,128)(2,1)} %bitcast.1), calls=%async_computation.1 | async-start | bytes 1572864 | tf_op jit(solution)/shard_map/all_to_all | solution.py:70
  29.1 11.8 %all-to-all-start = ((s32[16,1,32]{2,1,0:T(1,128)}), s32[16,1,32]{2,1,0:T(1,128)S(1)}, u32[]{:S(2)}, u32[]{:S(2)}) async-start(s32[16,1,32]{2,1,0:T(1,128)} %sub.39), calls=%async_computation | async-start | bytes 16384 | tf_op jit(solution)/shard_map/all_to_all | solution.py:77
  34.5 20.0 %collective-permute-start = (bf16[512,768]{1,0:T(8,128)(2,1)S(1)}, bf16[512,768]{1,0:T(8,128)(2,1)}, u32[]{:S(2)}, u32[]{:S(2)}) collective-permute-start(bf16[512,768]{1,0:T(8,128)(2,1)S(1)} %bitcast.7), channel_id=1, source_target_pairs={{0,1},{1,0},{2,3},{3,2},{4,5},{5,4},{6,7},{7,6},{8,9},{9,8},{10,11... | collective-permute-start | bytes 2359304 | tf_op jit(solution)/shard_map/ppermute | solution.py:13
  46.5 11.0 %copy-start.1 = (f32[129]{0:T(256)}, f32[129]{0:T(256)S(1)}, u32[]{:S(2)}) copy-start(f32[129]{0:T(256)S(1)} %scatter_custom_fusion.1) | copy-start | bytes 1552
  57.5 5.5 %slice-start = ((f32[129]{0:T(256)}), f32[128]{0:T(128)S(1)}, s32[]{:S(2)}) async-start(f32[129]{0:T(256)} %copy-done.1), calls=%async_computation.3 | async-start | bytes 1024 | tf_op jit(solution)/shard_map/slice | solution.py:44
